TPU v7x, 32 devices: a whole 2x2x4 slice. The times are simulated.
32 devices in a mesh: wide: 8 (over z, core), narrow: 4 (over y, x).
Axes of the slice: x: 2, y: 2, z: 4, core: 2. Of those that a mesh axis runs over, the one named last changes fastest.
Arguments:
- tokens: bfloat16 [8192, 2304], P(('wide', 'narrow')), may hold values from -6 to 6
- target: bfloat16 [8192, 2304], P(('wide', 'narrow')), may hold values from -6 to 6
- combine: bfloat16 [8192], P(('wide', 'narrow')), may hold values from 0.25 to 1
- filled: int32 [8], P('wide'), may hold values from 512 to 1024, as said below
- w_gate: bfloat16 [2304, 2048], P(None, 'narrow'), may hold values from -0.125 to 0.125
- w_up: bfloat16 [2304, 2048], P(None, 'narrow'), may hold values from -0.125 to 0.125
- w_down: bfloat16 [2048, 2304], P('narrow'), may hold values from -0.125 to 0.125
- momentum: float32 [8, 2048, 2304], P('wide', 'narrow'), may hold values from -6 to 6
Outputs:
- momentum_out: float32 [8, 2048, 2304], P('wide', 'narrow')
- update: bfloat16 [2048, 2304], P('narrow')
Inputs may be any that keep to these rules, and one draw needn't show every extreme that they name: `filled`: rows of a replica at or after its count are empty buffer slots; some replica's buffer is full in every draw.
All inputs are finite; a program needn't handle non-finite values.
Results may differ from a plain program's by a relative error of at most 0.015.
Values may be sent and summed in bfloat16 or wider, within the bound.
A program may use at most 128 MiB of HBM per device.

v0:
```python
import functools
import math

import jax
import jax.numpy as jnp
from jax import lax
from jax.experimental import pallas as pl
from jax.experimental.pallas import tpu as pltpu
from jax.sharding import PartitionSpec as P

SPAN = 64
BAND = 16
TILE = 256
BF = jnp.bfloat16
F32 = jnp.float32


def block_table(blocks):
    shape = (blocks * BAND, blocks * SPAN)
    row = lax.broadcasted_iota(jnp.int32, shape, 0)
    col = lax.broadcasted_iota(jnp.int32, shape, 1)
    freq = (row % BAND).astype(F32)
    cell = (col % SPAN).astype(F32)
    factor = jnp.where(row % BAND == 0, math.sqrt(1.0 / SPAN), math.sqrt(2.0 / SPAN))
    value = factor * jnp.cos(math.pi * (2.0 * cell + 1.0) * freq / (2.0 * SPAN))
    return jnp.where(row // BAND == col // SPAN, value, 0.0)


def halves(value):
    high = value.astype(BF)
    return high, (value - high.astype(F32)).astype(BF)


def dot3(left, right, contract):
    dims = (((contract[0],), (contract[1],)), ((), ()))
    dot = functools.partial(lax.dot_general, dimension_numbers=dims, preferred_element_type=F32)
    return dot(left[0], right[0]) + (dot(left[1], right[0]) + dot(left[0], right[1]))


def decode_tile(band_t, row_table, col_table):
    upper = dot3(halves(band_t), row_table, (1, 0))
    return dot3(halves(upper), col_table, (0, 0))


def grad_kernel(factor, hidden, error, momentum, row_h, row_l, col_h, col_l, residue, band):
    row_table = (row_h[...], row_l[...])
    col_table = (col_h[...], col_l[...])
    grad = lax.dot_general(
        hidden[...], error[...], (((0,), (0,)), ((), ())), preferred_element_type=F32
    )
    moved = 0.999 * momentum[0] + factor * grad
    squeezed = dot3(row_table, halves(moved), (1, 0))
    band_t = dot3(col_table, halves(squeezed), (1, 1))
    band[...] = band_t.astype(BF)
    residue[0] = moved - decode_tile(band_t, row_table, col_table)


def grad_step(hidden, error, momentum, tables, factor):
    rows, units = hidden.shape
    width = error.shape[1]
    tiles = width // TILE
    kept = units // SPAN * BAND
    kept_t = TILE // SPAN * BAND
    whole = lambda a: pl.BlockSpec(a.shape, lambda i: (0, 0))
    return pl.pallas_call(
        functools.partial(grad_kernel, factor),
        grid=(tiles,),
        in_specs=[
            whole(hidden),
            pl.BlockSpec((rows, TILE), lambda i: (0, i)),
            pl.BlockSpec((1, units, TILE), lambda i: (0, 0, i)),
        ]
        + [whole(t) for t in tables],
        out_specs=[
            pl.BlockSpec((1, units, TILE), lambda i: (0, 0, i)),
            pl.BlockSpec((kept_t, kept), lambda i: (i, 0)),
        ],
        out_shape=[
            jax.ShapeDtypeStruct((1, units, width), F32),
            jax.ShapeDtypeStruct((tiles * kept_t, kept), BF),
        ],
        name="grad_step",
    )(hidden, error, momentum, *tables)


def update_kernel(replicas, bands, row_h, row_l, col_h, col_l, update):
    total = jnp.sum(bands[...].astype(F32), axis=0)
    tile = decode_tile(total, (row_h[...], row_l[...]), (col_h[...], col_l[...]))
    update[...] = (tile * (1.0 / replicas)).astype(BF)


def update_step(bands, tables, units, width):
    replicas, rows_t, kept = bands.shape
    tiles = width // TILE
    whole = lambda a: pl.BlockSpec(a.shape, lambda i: (0, 0))
    return pl.pallas_call(
        functools.partial(update_kernel, replicas),
        grid=(tiles,),
        in_specs=[pl.BlockSpec((replicas, rows_t // tiles, kept), lambda i: (0, i, 0))]
        + [whole(t) for t in tables],
        out_specs=pl.BlockSpec((units, TILE), lambda i: (0, i)),
        out_shape=jax.ShapeDtypeStruct((units, width), BF),
        name="update_step",
    )(bands, *tables)


def make_tables(units):
    return halves(block_table(units // SPAN)) + halves(block_table(TILE // SPAN))


def forward(tokens, target, combine, filled, w_gate, w_up, w_down):
    local_rows = tokens.shape[0]
    piece = lax.all_gather(tokens, "narrow", axis=0, tiled=True)
    gate_proj = jnp.dot(piece, w_gate, preferred_element_type=F32)
    up_proj = jnp.dot(piece, w_up, preferred_element_type=F32)
    hidden = (jax.nn.silu(gate_proj) * up_proj).astype(BF)
    summed = lax.psum_scatter(
        jnp.dot(hidden, w_down, preferred_element_type=F32).astype(BF),
        "narrow",
        scatter_dimension=0,
        tiled=True,
    ).astype(F32)
    weight = combine.astype(F32)[:, None]
    row_ids = lax.axis_index("narrow") * local_rows + jnp.arange(local_rows, dtype=jnp.int32)
    error = jnp.where(
        (row_ids < filled[0])[:, None], weight * (weight * summed - target.astype(F32)), 0.0
    ).astype(BF)
    return hidden, lax.all_gather(error, "narrow", axis=0, tiled=True)


def body(tokens, target, combine, filled, w_gate, w_up, w_down, momentum):
    units, width = w_down.shape
    total_rows = tokens.shape[0] * lax.axis_size("narrow")
    tables = make_tables(units)
    hidden, errors = forward(tokens, target, combine, filled, w_gate, w_up, w_down)
    residue, band = grad_step(hidden, errors, momentum, tables, 1.0 / math.sqrt(total_rows))
    bands = lax.all_gather(band[None], "wide", axis=0, tiled=True)
    return residue, update_step(bands, tables, units, width)


def solution(mesh):
    in_specs = (
        P(("wide", "narrow"), None),
        P(("wide", "narrow"), None),
        P(("wide", "narrow")),
        P("wide"),
        P(None, "narrow"),
        P(None, "narrow"),
        P("narrow", None),
        P("wide", "narrow", None),
    )
    out_specs = (P("wide", "narrow", None), P("narrow", None))
    return jax.shard_map(body, mesh=mesh, in_specs=in_specs, out_specs=out_specs, check_vma=False)
```

profile of v0, /device:TPU:0, one launch (start us, length us, event | category | flops | bytes accessed | tf_op | source)
XLA Modules:
  0.0 258.1 jit_solution(1442317911627291251)
XLA Ops:
  7.2 0.0 copy-start
  7.2 0.0 all-gather.5.cloned.1.call-start
  7.2 0.7 all-gather.5.cloned.1.call-update
  7.9 0.0 reduce-scatter.2.cloned.1.call-start
  8.0 61.6 %all-gather.5.cloned.1.call-done = bf16[1024,2304]{1,0:T(8,128)(2,1)} async-done(((bf16[256,2304]{1,0:T(8,128)(2,1)}), bf16[1024,2304]{1,0:T(8,128)(2,1)}) %all-gather.5.cloned.1.call-update) | async-done | bytes 4718608 | tf_op jit(solution)/shard_map/all_gather | solution.py:113
  69.5 0.0 copy-start.3
  69.5 0.0 copy-start.4
  69.5 5.3 %fusion.20 = f32[1024,512]{1,0:T(8,128)S(1)} fusion(bf16[1024,2304]{1,0:T(8,128)(2,1)} %all-gather.5.cloned.1.call-done, bf16[2304,512]{1,0:T(8,128)(2,1)} %param.12), kind=kOutput, calls=%fused_computation.56 | convolution fusion | flops 2415919104 | bytes 9175040 | tf_op jit(solution)/shard_map/dot_general | solution.py:114
  74.8 0.0 copy-done.3
  74.9 0.0 copy-done.4
  74.9 2.8 %multiply_convert_fusion.hidden = bf16[1024,512]{1,0:T(8,128)(2,1)S(1)} fusion(f32[1024,512]{1,0:T(8,128)S(1)} %fusion.20, bf16[1024,2304]{1,0:T(8,128)(2,1)S(1)} %copy-done.3, bf16[2304,512]{1,0:T(8,128)(2,1)S(1)} %copy-done.4), kind=kOutput, calls=%fused_computation.2 | convolution fusion | flops 2419064832 | bytes 10223616 | tf_op jit(solution)/shard_map/dot_general | solution.py:115
  77.7 0.0 copy-start.2
  77.7 1.0 copy-done.2
  78.7 0.0 copy-done
  78.7 4.2 %convolution_convert_fusion = bf16[1024,2304]{1,0:T(8,128)(2,1)} fusion(bf16[1024,512]{1,0:T(8,128)(2,1)S(1)} %multiply_convert_fusion.hidden, bf16[512,2304]{1,0:T(8,128)(2,1)S(1)} %copy-done), kind=kOutput, calls=%fused_computation | convolution fusion | flops 2418278400 | bytes 8126464 | tf_op jit(solution)/shard_map/dot_general | solution.py:118
  82.9 0.0 copy-start.5
  82.9 0.0 copy-start.1
  82.9 0.0 reduce-scatter.2.cloned.1.call-update
  82.9 0.0 all-gather.7.cloned.1.call-start
  83.7 0.0 copy-done.5
  83.7 56.3 %reduce-scatter.2.cloned.1.call-done = bf16[256,2304]{1,0:T(8,128)(2,1)} async-done(((bf16[1024,2304]{1,0:T(8,128)(2,1)}), bf16[256,2304]{1,0:T(8,128)(2,1)}) %reduce-scatter.2.cloned.1.call-update) | async-done | bytes 1179664 | tf_op jit(solution)/shard_map/reduce_scatter | solution.py:117
  140.0 0.0 copy-done.1
  140.0 2.8 %select_convert_fusion = bf16[256,2304]{1,0:T(8,128)(2,1)} fusion(bf16[256,2304]{1,0:T(8,128)(2,1)S(1)} %copy-done.1, bf16[256,2304]{1,0:T(8,128)(2,1)} %reduce-scatter.2.cloned.1.call-done, f32[256]{0:T(256)S(1)} %convert_element_type.93, pred[256]{0:T(512)(128)(4,1)S(1)} %add_compare_fusion), kind=kLoop, calls=%fused_computation.1 | loop fusion | flops 4128768 | bytes 3540224 | tf_op jit(solution)/shard_map/convert_element_type | solution.py:127
  142.9 0.0 all-gather.7.cloned.1.call-update
  142.9 0.0 all-gather.9.cloned.1.call-start
  143.1 1.0 subtract_convert_fusion.1
  144.1 2.9 %subtract_convert_fusion = (bf16[128,512]{1,0:T(8,128)(2,1)}, bf16[128,512]{1,0:T(8,128)(2,1)}) fusion(s32[512]{0:T(512)S(1)} %get-tuple-element.11, s32[512]{0:T(512)S(1)} %get-tuple-element.12, s32[128]{0:T(128)S(1)} %get-tuple-element.19, s32[128]{0:T(128)S(1)} %get-tuple-element.20, s32[512]{0:T(512)S(1)} %get-tuple-element.10, ...), kind=kLoop, calls=%fused_computation.10 | loop fusion | flops 1310720 | bytes 273664 | tf_op jit(solution)/shard_map/convert_element_type | solution.py:31
  146.9 53.1 %all-gather.7.cloned.1.call-done.error = bf16[1024,2304]{1,0:T(8,128)(2,1)} async-done(((bf16[256,2304]{1,0:T(8,128)(2,1)}), bf16[1024,2304]{1,0:T(8,128)(2,1)}) %all-gather.7.cloned.1.call-update) | async-done | bytes 4718608 | tf_op jit(solution)/shard_map/all_gather | solution.py:128
  200.0 19.8 %grad_step.1 = (f32[1,512,2304]{2,1,0:T(8,128)}, bf16[576,128]{1,0:T(8,128)(2,1)}) custom-call(bf16[1024,512]{1,0:T(8,128)(2,1)} %copy-done.2, bf16[1024,2304]{1,0:T(8,128)(2,1)} %all-gather.7.cloned.1.call-done.error, f32[1,512,2304]{2,1,0:T(8,128)} %momentum.1, bf16[128,512]{1,0:T(8,128)(2,1)} %get-tuple-element.7.row_h, ...), custom_call_target="tpu_custom_call" | custom-call | tf_op jit(solution)/shard_map/grad_step/pallas_call | solution.py:65
  219.8 0.0 all-gather.9.cloned.1.call-update
  219.8 22.9 %all-gather.9.cloned.1.call-done = bf16[4608,128]{1,0:T(8,128)(2,1)} async-done(((bf16[576,128]{1,0:T(8,128)(2,1)}), bf16[4608,128]{1,0:T(8,128)(2,1)}) %all-gather.9.cloned.1.call-update) | async-done | bytes 1179664 | tf_op jit(solution)/shard_map/all_gather | solution.py:137
  242.7 8.8 %update_step.1 = bf16[512,2304]{1,0:T(8,128)(2,1)} custom-call(bf16[8,576,128]{2,1,0:T(8,128)(2,1)} %bitcast.9, bf16[128,512]{1,0:T(8,128)(2,1)} %get-tuple-element.7.row_h, bf16[128,512]{1,0:T(8,128)(2,1)} %get-tuple-element.6.row_l, bf16[64,256]{1,0:T(8,128)(2,1)} %get-tuple-element.9.col_h, bf16[64,256]{1,0:T(8,128)(2,1)} %get-tuple-element.8.col_l), custom_call_target="tpu_custom_call" | custom-call | tf_op jit(solution)/shard_map/update_step/pallas_call | solution.py:96
  (14 shorter events, 0.1 us)
Async XLA Ops:
  7.2 71.5 %copy-start = (bf16[512,2304]{1,0:T(8,128)(2,1)S(1)}, bf16[512,2304]{1,0:T(8,128)(2,1)}, u32[]{:S(2)}) copy-start(bf16[512,2304]{1,0:T(8,128)(2,1)} %param.14) | copy-start | bytes 7077892
  7.2 62.3 %all-gather.5.cloned.1.call-start = ((), (), s32[]{:S(2)}) async-start(), calls=%async_computation.1 | async-start | bytes 5898240 | tf_op jit(solution)/shard_map/all_gather | solution.py:113
  7.9 132.1 %reduce-scatter.2.cloned.1.call-start = ((), (), s32[]{:S(2)}) async-start(), calls=%async_computation.2 | async-start | bytes 5898240 | tf_op jit(solution)/shard_map/reduce_scatter | solution.py:117
  69.5 5.3 %copy-start.3 = (bf16[1024,2304]{1,0:T(8,128)(2,1)S(1)}, bf16[1024,2304]{1,0:T(8,128)(2,1)}, u32[]{:S(2)}) copy-start(bf16[1024,2304]{1,0:T(8,128)(2,1)} %all-gather.5.cloned.1.call-done) | copy-start | bytes 14155780
  69.5 5.3 %copy-start.4 = (bf16[2304,512]{1,0:T(8,128)(2,1)S(1)}, bf16[2304,512]{1,0:T(8,128)(2,1)}, u32[]{:S(2)}) copy-start(bf16[2304,512]{1,0:T(8,128)(2,1)} %param.13) | copy-start | bytes 7077892
  77.7 1.0 copy-start.2
  82.9 0.8 copy-start.5
  82.9 57.1 %copy-start.1 = (bf16[256,2304]{1,0:T(8,128)(2,1)S(1)}, bf16[256,2304]{1,0:T(8,128)(2,1)}, u32[]{:S(2)}) copy-start(bf16[256,2304]{1,0:T(8,128)(2,1)} %param.9) | copy-start | bytes 3538948
  82.9 117.1 %all-gather.7.cloned.1.call-start = ((), (), s32[]{:S(2)}) async-start(), calls=%async_computation.3 | async-start | bytes 5898240 | tf_op jit(solution)/shard_map/all_gather | solution.py:128
  142.9 99.8 %all-gather.9.cloned.1.call-start = ((), (), s32[]{:S(2)}) async-start(), calls=%async_computation.4 | async-start | bytes 1327104 | tf_op jit(solution)/shard_map/all_gather | solution.py:137
Sparse Core Ops, SparseCore 0:
  9.8 59.6 all-gather.4
  83.0 56.9 reduce-scatter.1
  143.0 56.9 all-gather.6
  219.9 22.7 all-gather.8
where the time goes:
time: 258 us
  waiting for transfers between devices  195 us (76%)
  Pallas kernels  28.5 us (11%)
  between operations  14.7 us (6%)
  matrix products  12.3 us (5%)
  other arithmetic  6.76 us (3%)
    all_gather x1, waiting for transfers between devices, forward(): piece = lax.all_gather(tokens, 'narrow', axis=0, tiled=True)  61.6 us
    reduce_scatter x1, waiting for transfers between devices, forward(): lax.psum_scatter(jnp.dot(hidden, w_down, preferred_element_type=F32).asty...  56.3 us
    all_gather x1, waiting for transfers between devices, forward(): return (hidden, lax.all_gather(error, 'narrow', axis=0, tiled=True))  53.1 us
    all_gather x1, waiting for transfers between devices, body(): bands = lax.all_gather(band[None], 'wide', axis=0, tiled=True)  22.9 us
    pallas_call x1, Pallas kernels, grad_step(): pl.pallas_call(functools.partial(grad_kernel, factor), grid=(tiles,), in_...  19.8 us
    pallas_call x1, Pallas kernels, update_step(): pl.pallas_call(functools.partial(update_kernel, replicas), grid=(tiles,),...  8.79 us
    dot_general x1, matrix products, forward(): gate_proj = jnp.dot(piece, w_gate, preferred_element_type=F32)  5.31 us
  transfers between devices with their start and end apart: 4, of which 4 were waited for; matrix products, arithmetic and copies ran while one was open for 2% of the time, Pallas kernels for 0%

commit v1 on v0

v1 whole, which is shorter than its diff:
```python
import functools
import math

import jax
import jax.numpy as jnp
from jax import lax
from jax.experimental import pallas as pl
from jax.experimental.pallas import tpu as pltpu
from jax.sharding import PartitionSpec as P

SPAN = 64
BAND = 16
TILE = 256
BF = jnp.bfloat16
F32 = jnp.float32


def block_table(blocks):
    shape = (blocks * BAND, blocks * SPAN)
    row = lax.broadcasted_iota(jnp.int32, shape, 0)
    col = lax.broadcasted_iota(jnp.int32, shape, 1)
    freq = (row % BAND).astype(F32)
    cell = (col % SPAN).astype(F32)
    factor = jnp.where(row % BAND == 0, math.sqrt(1.0 / SPAN), math.sqrt(2.0 / SPAN))
    value = factor * jnp.cos(math.pi * (2.0 * cell + 1.0) * freq / (2.0 * SPAN))
    return jnp.where(row // BAND == col // SPAN, value, 0.0)


def halves(value):
    high = value.astype(BF)
    return high, (value - high.astype(F32)).astype(BF)


def dot3(left, right, contract):
    dims = (((contract[0],), (contract[1],)), ((), ()))
    dot = functools.partial(lax.dot_general, dimension_numbers=dims, preferred_element_type=F32)
    return dot(left[0], right[0]) + (dot(left[1], right[0]) + dot(left[0], right[1]))


def decode_tile(band, tables):
    wide = dot3(halves(band), halves(tables[3][...]), (1, 0))
    return dot3(halves(tables[1][...]), halves(wide), (1, 0))


def grad_kernel(factor, hidden_t, error, momentum, *refs):
    tables, (residue, band_t) = refs[:4], refs[4:]
    grad = jnp.dot(hidden_t[...], error[...], preferred_element_type=F32)
    moved = 0.999 * momentum[0] + factor * grad
    squeezed = dot3(halves(tables[0][...]), halves(moved), (1, 0))
    band = dot3(halves(squeezed), halves(tables[2][...]), (1, 0))
    band_t[...] = band.T
    residue[0] = moved - decode_tile(band, tables)


def whole(a):
    return pl.BlockSpec(a.shape, lambda i: (0,) * a.ndim)


def grad_step(hidden_t, error, momentum, tables, factor):
    units, rows = hidden_t.shape
    width = error.shape[1]
    tiles = width // TILE
    kept = units // SPAN * BAND
    kept_t = TILE // SPAN * BAND
    return pl.pallas_call(
        functools.partial(grad_kernel, factor),
        grid=(tiles,),
        in_specs=[
            whole(hidden_t),
            pl.BlockSpec((rows, TILE), lambda i: (0, i)),
            pl.BlockSpec((1, units, TILE), lambda i: (0, 0, i)),
        ]
        + [whole(t) for t in tables],
        out_specs=[
            pl.BlockSpec((1, units, TILE), lambda i: (0, 0, i)),
            pl.BlockSpec((kept_t, kept), lambda i: (i, 0)),
        ],
        out_shape=[
            jax.ShapeDtypeStruct((1, units, width), F32),
            jax.ShapeDtypeStruct((tiles * kept_t, kept), F32),
        ],
        name="grad_step",
    )(hidden_t, error, momentum, *tables)


def update_kernel(replicas, bands, *refs):
    tables, update = refs[:4], refs[4]
    update[...] = (decode_tile(bands[...].T, tables) * (1.0 / replicas)).astype(BF)


def update_step(bands, tables, units, width, replicas):
    rows_t, kept = bands.shape
    tiles = width // TILE
    return pl.pallas_call(
        functools.partial(update_kernel, replicas),
        grid=(tiles,),
        in_specs=[pl.BlockSpec((rows_t // tiles, kept), lambda i: (i, 0))]
        + [whole(t) for t in tables],
        out_specs=pl.BlockSpec((units, TILE), lambda i: (0, i)),
        out_shape=jax.ShapeDtypeStruct((units, width), BF),
        name="update_step",
    )(bands, *tables)


def make_tables(units):
    left = block_table(units // SPAN)
    right = block_table(TILE // SPAN)
    return left, left.T, right.T, right


def remote(src, dst, send, recv, index, axis, peer):
    return pltpu.make_async_remote_copy(
        src_ref=src,
        dst_ref=dst,
        send_sem=send.at[index],
        recv_sem=recv.at[index],
        device_id={axis: peer},
        device_id_type=pl.DeviceIdType.MESH,
    )


def greet(axis, peers):
    barrier = pltpu.get_barrier_semaphore()
    for peer in peers:
        pl.semaphore_signal(
            barrier, inc=1, device_id={axis: peer}, device_id_type=pl.DeviceIdType.MESH
        )
    pl.semaphore_wait(barrier, len(peers))


def square_kernel(
    tokens, target, weight, live, gate_hbm, up_hbm, down_hbm, hidden_out, error_out,
    gate, up, down, held, part, errors, from_x, from_y, relay_x, relay_y, hidden_t, hidden,
    send, recv, local,
):
    me = lax.axis_index("narrow")
    x_peer = me + 1 - 2 * (me % 2)
    y_peer = (me + 2) % 4
    rows, width = tokens.shape
    units = down.shape[0]
    half = rows // 2
    top, low = pl.ds(0, half), pl.ds(half, half)

    loads = [
        pltpu.make_async_copy(s, t, local.at[i])
        for i, (s, t) in enumerate(((gate_hbm, gate), (up_hbm, up), (down_hbm, down)))
    ]
    for load in loads:
        load.start()
    greet("narrow", (x_peer, y_peer))

    def spread(own, slots, base):
        copies = [
            remote(own.at[top], slots.at[0, top], send, recv, base, "narrow", x_peer),
            remote(own.at[low], slots.at[1, low], send, recv, base + 1, "narrow", y_peer),
            remote(own.at[low], slots.at[0, low], send, recv, base + 2, "narrow", x_peer),
            remote(own.at[top], slots.at[1, top], send, recv, base + 3, "narrow", y_peer),
            remote(slots.at[0, top], slots.at[2, top], send, recv, base + 4, "narrow", y_peer),
            remote(slots.at[1, low], slots.at[2, low], send, recv, base + 5, "narrow", x_peer),
        ]
        for copy in copies[:4]:
            copy.start()
        return copies

    def pass_on(copies):
        copies[0].wait_recv()
        copies[4].start()
        copies[1].wait_recv()
        copies[5].start()

    def expert(source, slot):
        @pl.loop(0, units // TILE)
        def _(c):
            at = pl.ds(pl.multiple_of(c * TILE, TILE), TILE)
            block = source[...]
            gated = jnp.dot(block, gate[:, at], preferred_element_type=F32)
            raised = jnp.dot(block, up[:, at], preferred_element_type=F32)
            value = gated / (1.0 + jnp.exp(-gated)) * raised
            hidden[:, at] = value.astype(BF)
            hidden_t[at, slot * rows : (slot + 1) * rows] = value.T.astype(BF)

        @pl.loop(0, width // TILE)
        def _(c):
            at = pl.ds(pl.multiple_of(c * TILE, TILE), TILE)
            part[slot, :, at] = jnp.dot(
                hidden[...], down[:, at], preferred_element_type=F32
            ).astype(BF)

    gathers = spread(tokens, held, 0)
    for load in loads:
        load.wait()
    expert(tokens, 0)
    pass_on(gathers)
    gathers[2].wait_recv()
    expert(held.at[0], 1)
    sums = [
        remote(part.at[3, top], relay_y, send, recv, 6, "narrow", x_peer),
        remote(part.at[3, low], relay_x, send, recv, 7, "narrow", y_peer),
        remote(part.at[1, top], from_x.at[top], send, recv, 8, "narrow", x_peer),
        remote(part.at[2, low], from_y.at[low], send, recv, 9, "narrow", y_peer),
        remote(part.at[1, low], from_x.at[low], send, recv, 10, "narrow", x_peer),
        remote(part.at[2, top], from_y.at[top], send, recv, 11, "narrow", y_peer),
    ]
    sums[2].start()
    gathers[3].wait_recv()
    expert(held.at[1], 2)
    sums[3].start()
    gathers[4].wait_recv()
    gathers[5].wait_recv()
    expert(held.at[2], 3)
    sums[0].start()
    sums[1].start()
    hidden_store = pltpu.make_async_copy(hidden_t, hidden_out, local.at[3])
    hidden_store.start()

    step = 16

    def add_rows(slot, first, arrived):
        @pl.loop(0, half // step)
        def _(c):
            mine = pl.ds(pl.multiple_of(first + c * step, step), step)
            theirs = pl.ds(pl.multiple_of(c * step, step), step)
            part[slot, mine, :] = (
                part[slot, mine, :].astype(F32) + arrived[theirs, :].astype(F32)
            ).astype(BF)

    def error_rows(first):
        @pl.loop(0, half // step)
        def _(c):
            at = pl.ds(pl.multiple_of(first + c * step, step), step)
            total = (
                part[0, at, :].astype(F32)
                + from_x[at, :].astype(F32)
                + from_y[at, :].astype(F32)
            )
            scale = weight[at, :]
            value = scale * (scale * total - target[at, :].astype(F32))
            errors[0, at, :] = jnp.where(live[at, :] > 0.0, value, 0.0).astype(BF)

    sums[0].wait_recv()
    add_rows(2, 0, relay_y)
    sums[5].start()
    sums[1].wait_recv()
    add_rows(1, half, relay_x)
    sums[4].start()
    sums[2].wait_recv()
    sums[5].wait_recv()
    error_rows(0)
    sums[3].wait_recv()
    sums[4].wait_recv()
    error_rows(half)
    shared = spread(errors.at[0], errors.at[pl.ds(1, 3)], 12)
    stores = [
        pltpu.make_async_copy(errors.at[i], error_out.at[i], local.at[4 + i]) for i in range(4)
    ]
    stores[0].start()
    pass_on(shared)
    shared[2].wait_recv()
    stores[1].start()
    shared[3].wait_recv()
    stores[2].start()
    shared[4].wait_recv()
    shared[5].wait_recv()
    stores[3].start()
    for copy in gathers + sums + shared:
        copy.wait_send()
    hidden_store.wait()
    for store in stores:
        store.wait()


def square_forward(tokens, target, combine, filled, w_gate, w_up, w_down):
    rows, width = tokens.shape
    units = w_down.shape[0]
    half = rows // 2
    row_ids = lax.axis_index("narrow") * rows + jnp.arange(rows, dtype=jnp.int32)
    live = (row_ids < filled[0]).astype(F32)[:, None]
    weight = combine.astype(F32)[:, None]
    vmem = pl.BlockSpec(memory_space=pltpu.VMEM)
    hbm = pl.BlockSpec(memory_space=pl.ANY)
    block = lambda *shape: pltpu.VMEM(shape, BF)
    hidden_t, errors = pl.pallas_call(
        square_kernel,
        in_specs=[vmem] * 4 + [hbm] * 3,
        out_specs=[hbm] * 2,
        out_shape=[
            jax.ShapeDtypeStruct((units, 4 * rows), BF),
            jax.ShapeDtypeStruct((4, rows, width), BF),
        ],
        scratch_shapes=[
            block(width, units), block(width, units), block(units, width),
            block(3, rows, width), block(4, rows, width), block(4, rows, width),
            block(rows, width), block(rows, width), block(half, width), block(half, width),
            block(units, 4 * rows), block(rows, units),
            pltpu.SemaphoreType.DMA((18,)), pltpu.SemaphoreType.DMA((18,)),
            pltpu.SemaphoreType.DMA((8,)),
        ],
        compiler_params=pltpu.CompilerParams(
            collective_id=0, has_side_effects=True, vmem_limit_bytes=60 << 20
        ),
        name="square_forward",
    )(tokens, target, weight, live, w_gate, w_up, w_down)
    return hidden_t, errors.reshape(4 * rows, width)


def band_kernel(count, band, total, outgoing, arrived, summed, gathered, send, recv):
    me = lax.axis_index("wide")
    peers = [(me + k) % count for k in range(1, count)]
    greet("wide", peers)
    share = band.shape[0] // count
    outgoing[...] = band[...].reshape(count, share, band.shape[1]).astype(BF)
    first = [
        remote(outgoing.at[p], arrived.at[k], send, recv, k, "wide", p)
        for k, p in enumerate(peers)
    ]
    for copy in first:
        copy.start()
    amount = outgoing[me].astype(F32)
    for k, copy in enumerate(first):
        copy.wait_recv()
        amount = amount + arrived[k].astype(F32)
    summed[...] = amount.astype(BF)
    second = [
        remote(summed, gathered.at[me], send, recv, count + k, "wide", p)
        for k, p in enumerate(peers)
    ]
    for copy in second:
        copy.start()
    for copy in second:
        copy.wait_recv()
    for copy in first + second:
        copy.wait_send()
    gathered[me] = summed[...]
    total[...] = gathered[...].astype(F32).reshape(band.shape)


def band_sum(band, count):
    share = band.shape[0] // count
    vmem = pl.BlockSpec(memory_space=pltpu.VMEM)
    block = lambda *shape: pltpu.VMEM(shape + (share, band.shape[1]), BF)
    return pl.pallas_call(
        functools.partial(band_kernel, count),
        in_specs=[vmem],
        out_specs=vmem,
        out_shape=jax.ShapeDtypeStruct(band.shape, F32),
        scratch_shapes=[
            block(count), block(count - 1), block(), block(count),
            pltpu.SemaphoreType.DMA((2 * count,)), pltpu.SemaphoreType.DMA((2 * count,)),
        ],
        compiler_params=pltpu.CompilerParams(collective_id=1, has_side_effects=True),
        name="band_sum",
    )(band)


def forward(tokens, target, combine, filled, w_gate, w_up, w_down):
    local_rows = tokens.shape[0]
    piece = lax.all_gather(tokens, "narrow", axis=0, tiled=True)
    gate_proj = jnp.dot(piece, w_gate, preferred_element_type=F32)
    up_proj = jnp.dot(piece, w_up, preferred_element_type=F32)
    hidden = (jax.nn.silu(gate_proj) * up_proj).astype(BF)
    summed = lax.psum_scatter(
        jnp.dot(hidden, w_down, preferred_element_type=F32).astype(BF),
        "narrow",
        scatter_dimension=0,
        tiled=True,
    ).astype(F32)
    weight = combine.astype(F32)[:, None]
    row_ids = lax.axis_index("narrow") * local_rows + jnp.arange(local_rows, dtype=jnp.int32)
    error = jnp.where(
        (row_ids < filled[0])[:, None], weight * (weight * summed - target.astype(F32)), 0.0
    ).astype(BF)
    return hidden.T, lax.all_gather(error, "narrow", axis=0, tiled=True)


def body(tokens, target, combine, filled, w_gate, w_up, w_down, momentum):
    units, width = w_down.shape
    narrow, replicas = lax.axis_size("narrow"), lax.axis_size("wide")
    total_rows = tokens.shape[0] * narrow
    tables = make_tables(units)
    step = square_forward if narrow == 4 else forward
    hidden_t, errors = step(tokens, target, combine, filled, w_gate, w_up, w_down)
    residue, band = grad_step(hidden_t, errors, momentum, tables, 1.0 / math.sqrt(total_rows))
    if narrow == 4:
        total = band_sum(band, replicas)
    else:
        bands = lax.all_gather(band.astype(BF)[None], "wide", axis=0, tiled=True)
        total = jnp.sum(bands.astype(F32), axis=0)
    return residue, update_step(total, tables, units, width, replicas)


def solution(mesh):
    in_specs = (
        P(("wide", "narrow"), None),
        P(("wide", "narrow"), None),
        P(("wide", "narrow")),
        P("wide"),
        P(None, "narrow"),
        P(None, "narrow"),
        P("narrow", None),
        P("wide", "narrow", None),
    )
    out_specs = (P("wide", "narrow", None), P("narrow", None))
    return jax.shard_map(body, mesh=mesh, in_specs=in_specs, out_specs=out_specs, check_vma=False)
```

time: 258 us -> 178 us (0.69)
  waiting for transfers between devices: 195 us -> 0 us
  Pallas kernels: 28.5 us -> 167 us
  between operations: 14.7 us -> 1.36 us
  matrix products: 12.3 us -> 0 us
    pallas_call x0 -> x2, Pallas kernels: none -> 139 us  [the longest x1 125 us: square_forward(): pl.pallas_call(square_kernel, in_specs=[vmem] * 4 + [hbm] * 3, out_specs=...]
    all_gather x3 -> x0, waiting for transfers between devices: 138 us -> none  [the longest x1 61.6 us: forward(): piece = lax.all_gather(tokens, 'narrow', axis=0, tiled=True)]
    reduce_scatter x1 -> x0, waiting for transfers between devices: 56.3 us -> none  [forward(): lax.psum_scatter(jnp.dot(hidden, w_down, preferred_element_type=F32).asty...]
    dot_general x3 -> x0, matrix products: 12.3 us -> none  [the longest x1 5.31 us: forward(): gate_proj = jnp.dot(piece, w_gate, preferred_element_type=F32)]
    select_n x0 -> x4, other arithmetic: none -> 7.31 us  [block_table(): return jnp.where(row // BAND == col // SPAN, value, 0.0)]
    convert_element_type x4 -> x1, other arithmetic: 6.69 us -> 0.67 us  [square_forward(): live = (row_ids < filled[0]).astype(F32)[:, None]]
  transfers between devices with their start and end apart: 4 -> 0, of which waited for: 4 -> 0; matrix products, arithmetic and copies ran while one was open for 2% -> 0% of each run, Pallas kernels for 0% -> 0%
where the time goes in v1:
time: 178 us; the launch traced here: 177 us
  Pallas kernels  167 us (94%)
  other arithmetic  8.71 us (5%)
    pallas_call x1, Pallas kernels, square_forward(): pl.pallas_call(square_kernel, in_specs=[vmem] * 4 + [hbm] * 3, out_specs=...  125 us
    pallas_call x1, Pallas kernels, grad_step(): pl.pallas_call(functools.partial(grad_kernel, factor), grid=(tiles,), in_...  18.8 us
    pallas_call x1, Pallas kernels, band_sum(): pl.pallas_call(functools.partial(band_kernel, count), in_specs=[vmem], ou...  14.6 us
    pallas_call x1, Pallas kernels, update_step(): pl.pallas_call(functools.partial(update_kernel, replicas), grid=(tiles,),...  8.54 us
    select_n x4, other arithmetic, block_table(): return jnp.where(row // BAND == col // SPAN, value, 0.0)  7.31 us

profile of v1, /device:TPU:0, one launch (start us, length us, event | category | flops | bytes accessed | tf_op | source)
XLA Modules:
  0.0 177.4 jit_solution(12928458789989707617)
XLA Ops:
  1.3 0.7 broadcast_in_dim.56
  2.1 1.0 fusion.20.refs_3_
  3.0 1.3 fusion.14.refs_2_
  4.4 0.8 copy.12.weight
  5.2 0.7 fusion.15.live
  5.8 2.9 %fusion.4.refs_0_ = f32[128,512]{1,0:T(8,128)} fusion(s32[512]{0:T(512)S(1)} %get-tuple-element.11, s32[512]{0:T(512)S(1)} %get-tuple-element.12, s32[128]{0:T(128)S(1)} %get-tuple-element.19, s32[128]{0:T(128)S(1)} %get-tuple-element.20, s32[512]{0:T(512)S(1)} %get-tuple-element.10, s32[512]{0:T(512)S(1)} %get-tuple-element.13, ...), kind=kLoop, calls=%fused_computation.8 | loop fusion | flops 1048576 | bytes 273664 | tf_op jit(solution)/shard_map/jit(_where)/select_n | solution.py:26
  8.7 2.1 %fusion.9.refs_1_ = f32[512,128]{1,0:T(8,128)} fusion(s32[512]{0:T(512)S(1)} %get-tuple-element.11, s32[512]{0:T(512)S(1)} %get-tuple-element.12, s32[128]{0:T(128)S(1)} %get-tuple-element.19, s32[128]{0:T(128)S(1)} %get-tuple-element.20, s32[512]{0:T(512)S(1)} %get-tuple-element.10, s32[512]{0:T(512)S(1)} %get-tuple-element.13, ...), kind=kLoop, calls=%fused_computation.13 | loop fusion | flops 1048576 | bytes 273664 | tf_op jit(solution)/shard_map/jit(_where)/select_n | solution.py:26
  10.8 124.6 %square_forward.1 = (bf16[512,1024]{1,0:T(8,128)(2,1)}, bf16[4,256,2304]{2,1,0:T(8,128)(2,1)}) custom-call(bf16[256,2304]{1,0:T(8,128)(2,1)} %tokens.1, bf16[256,2304]{1,0:T(8,128)(2,1)} %target.1, f32[256,1]{1,0:T(8,128)} %copy.12.weight, f32[256,1]{1,0:T(8,128)} %fusion.15.live, bf16[2304,512]{1,0:T(8,128)(2,1)} %gate_hbm.1, bf16[2304,512]{1,0:T(8,128)(2,1)} %up_hbm.1, ...), custom_call_target="tpu_custom_call" | custom-call | tf_op jit(solution)/shard_map/square_forward/pallas_call | solution.py:282
  135.4 18.8 %grad_step.1 = (f32[1,512,2304]{2,1,0:T(8,128)}, f32[576,128]{1,0:T(8,128)}) custom-call(bf16[512,1024]{1,0:T(8,128)(2,1)} %get-tuple-element.6.hidden_t, bf16[1024,2304]{1,0:T(8,128)(2,1)} %bitcast.4, f32[1,512,2304]{2,1,0:T(8,128)} %momentum.1, f32[128,512]{1,0:T(8,128)} %fusion.4.refs_0_, f32[512,128]{1,0:T(8,128)} %fusion.9.refs_1_, ...), custom_call_target="tpu_custom_call" | custom-call | tf_op jit(solution)/shard_map/grad_step/pallas_call | solution.py:65
  154.2 14.6 %band_sum.1.bands = f32[576,128]{1,0:T(8,128)} custom-call(f32[576,128]{1,0:T(8,128)} %get-tuple-element.9.band), custom_call_target="tpu_custom_call" | custom-call | tf_op jit(solution)/shard_map/band_sum/pallas_call | solution.py:341
  168.8 8.5 %update_step.1 = bf16[512,2304]{1,0:T(8,128)(2,1)} custom-call(f32[576,128]{1,0:T(8,128)} %band_sum.1.bands, f32[128,512]{1,0:T(8,128)} %fusion.4.refs_0_, f32[512,128]{1,0:T(8,128)} %fusion.9.refs_1_, f32[256,64]{1,0:T(8,128)} %fusion.14.refs_2_, f32[64,256]{1,0:T(8,128)} %fusion.20.refs_3_), custom_call_target="tpu_custom_call" | custom-call | tf_op jit(solution)/shard_map/update_step/pallas_call | solution.py:94
  (12 shorter events, 0.1 us)

commit v2 on v1

--- a/solution.py
+++ b/solution.py
@@ -3,6 +3,7 @@
 
 import jax
 import jax.numpy as jnp
+import numpy as np
 from jax import lax
 from jax.experimental import pallas as pl
 from jax.experimental.pallas import tpu as pltpu
@@ -16,14 +17,11 @@
 
 
 def block_table(blocks):
-    shape = (blocks * BAND, blocks * SPAN)
-    row = lax.broadcasted_iota(jnp.int32, shape, 0)
-    col = lax.broadcasted_iota(jnp.int32, shape, 1)
-    freq = (row % BAND).astype(F32)
-    cell = (col % SPAN).astype(F32)
-    factor = jnp.where(row % BAND == 0, math.sqrt(1.0 / SPAN), math.sqrt(2.0 / SPAN))
-    value = factor * jnp.cos(math.pi * (2.0 * cell + 1.0) * freq / (2.0 * SPAN))
-    return jnp.where(row // BAND == col // SPAN, value, 0.0)
+    row = np.arange(blocks * BAND)[:, None]
+    col = np.arange(blocks * SPAN)[None, :]
+    factor = np.where(row % BAND == 0, math.sqrt(1.0 / SPAN), math.sqrt(2.0 / SPAN))
+    value = factor * np.cos(math.pi * (2.0 * (col % SPAN) + 1.0) * (row % BAND) / (2.0 * SPAN))
+    return np.where(row // BAND == col // SPAN, value, 0.0).astype(np.float32)
 
 
 def halves(value):
@@ -38,18 +36,26 @@
 
 
 def decode_tile(band, tables):
-    wide = dot3(halves(band), halves(tables[3][...]), (1, 0))
-    return dot3(halves(tables[1][...]), halves(wide), (1, 0))
-
-
-def grad_kernel(factor, hidden_t, error, momentum, *refs):
-    tables, (residue, band_t) = refs[:4], refs[4:]
-    grad = jnp.dot(hidden_t[...], error[...], preferred_element_type=F32)
-    moved = 0.999 * momentum[0] + factor * grad
-    squeezed = dot3(halves(tables[0][...]), halves(moved), (1, 0))
-    band = dot3(halves(squeezed), halves(tables[2][...]), (1, 0))
-    band_t[...] = band.T
-    residue[0] = moved - decode_tile(band, tables)
+    wide = dot3(halves(band), tables[3], (1, 0))
+    return dot3(tables[1], halves(wide), (1, 0))
+
+
+def read_tables(refs):
+    return [(refs[2 * k][...], refs[2 * k + 1][...]) for k in range(4)]
+
+
+def grad_kernel(factor, subs, hidden_t, error, momentum, *refs):
+    residue, band_t = refs[8:]
+    tables = read_tables(refs)
+    kept_t = TILE // SPAN * BAND
+    for k in range(subs):
+        at = slice(k * TILE, (k + 1) * TILE)
+        grad = jnp.dot(hidden_t[...], error[:, at], preferred_element_type=F32)
+        moved = 0.999 * momentum[0, :, at] + factor * grad
+        squeezed = dot3(tables[0], halves(moved), (1, 0))
+        band = dot3(halves(squeezed), tables[2], (1, 0))
+        band_t[k * kept_t : (k + 1) * kept_t, :] = band.T
+        residue[0, :, at] = moved - decode_tile(band, tables)
 
 
 def whole(a):
@@ -59,20 +65,22 @@
 def grad_step(hidden_t, error, momentum, tables, factor):
     units, rows = hidden_t.shape
     width = error.shape[1]
-    tiles = width // TILE
+    subs = 3 if width // TILE % 3 == 0 else 1
+    step = TILE * subs
+    tiles = width // step
     kept = units // SPAN * BAND
-    kept_t = TILE // SPAN * BAND
+    kept_t = step // SPAN * BAND
     return pl.pallas_call(
-        functools.partial(grad_kernel, factor),
+        functools.partial(grad_kernel, factor, subs),
         grid=(tiles,),
         in_specs=[
             whole(hidden_t),
-            pl.BlockSpec((rows, TILE), lambda i: (0, i)),
-            pl.BlockSpec((1, units, TILE), lambda i: (0, 0, i)),
+            pl.BlockSpec((rows, step), lambda i: (0, i)),
+            pl.BlockSpec((1, units, step), lambda i: (0, 0, i)),
         ]
         + [whole(t) for t in tables],
         out_specs=[
-            pl.BlockSpec((1, units, TILE), lambda i: (0, 0, i)),
+            pl.BlockSpec((1, units, step), lambda i: (0, 0, i)),
             pl.BlockSpec((kept_t, kept), lambda i: (i, 0)),
         ],
         out_shape=[
@@ -83,20 +91,27 @@
     )(hidden_t, error, momentum, *tables)
 
 
-def update_kernel(replicas, bands, *refs):
-    tables, update = refs[:4], refs[4]
-    update[...] = (decode_tile(bands[...].T, tables) * (1.0 / replicas)).astype(BF)
+def update_kernel(replicas, subs, bands, *refs):
+    update = refs[8]
+    tables = read_tables(refs)
+    kept_t = TILE // SPAN * BAND
+    for k in range(subs):
+        band = bands[k * kept_t : (k + 1) * kept_t, :].T
+        tile = decode_tile(band, tables) * (1.0 / replicas)
+        update[:, k * TILE : (k + 1) * TILE] = tile.astype(BF)
 
 
 def update_step(bands, tables, units, width, replicas):
     rows_t, kept = bands.shape
-    tiles = width // TILE
+    subs = 3 if width // TILE % 3 == 0 else 1
+    step = TILE * subs
+    tiles = width // step
     return pl.pallas_call(
-        functools.partial(update_kernel, replicas),
+        functools.partial(update_kernel, replicas, subs),
         grid=(tiles,),
         in_specs=[pl.BlockSpec((rows_t // tiles, kept), lambda i: (i, 0))]
         + [whole(t) for t in tables],
-        out_specs=pl.BlockSpec((units, TILE), lambda i: (0, i)),
+        out_specs=pl.BlockSpec((units, step), lambda i: (0, i)),
         out_shape=jax.ShapeDtypeStruct((units, width), BF),
         name="update_step",
     )(bands, *tables)
@@ -105,7 +120,11 @@
 def make_tables(units):
     left = block_table(units // SPAN)
     right = block_table(TILE // SPAN)
-    return left, left.T, right.T, right
+    pieces = []
+    for table in (left, left.T, right.T, right):
+        high = table.astype(BF)
+        pieces += [high, (table - high.astype(np.float32)).astype(BF)]
+    return [jnp.asarray(np.ascontiguousarray(p)) for p in pieces]
 
 
 def remote(src, dst, send, recv, index, axis, peer):
@@ -129,7 +148,7 @@
 
 
 def square_kernel(
-    tokens, target, weight, live, gate_hbm, up_hbm, down_hbm, hidden_out, error_out,
+    tokens, target, weight, gate_hbm, up_hbm, down_hbm, hidden_out, error_out,
     gate, up, down, held, part, errors, from_x, from_y, relay_x, relay_y, hidden_t, hidden,
     send, recv, local,
 ):
@@ -235,7 +254,7 @@
             )
             scale = weight[at, :]
             value = scale * (scale * total - target[at, :].astype(F32))
-            errors[0, at, :] = jnp.where(live[at, :] > 0.0, value, 0.0).astype(BF)
+            errors[0, at, :] = value.astype(BF)
 
     sums[0].wait_recv()
     add_rows(2, 0, relay_y)
@@ -274,14 +293,13 @@
     units = w_down.shape[0]
     half = rows // 2
     row_ids = lax.axis_index("narrow") * rows + jnp.arange(rows, dtype=jnp.int32)
-    live = (row_ids < filled[0]).astype(F32)[:, None]
-    weight = combine.astype(F32)[:, None]
+    weight = jnp.where(row_ids < filled[0], combine.astype(F32), 0.0)[:, None]
     vmem = pl.BlockSpec(memory_space=pltpu.VMEM)
     hbm = pl.BlockSpec(memory_space=pl.ANY)
     block = lambda *shape: pltpu.VMEM(shape, BF)
     hidden_t, errors = pl.pallas_call(
         square_kernel,
-        in_specs=[vmem] * 4 + [hbm] * 3,
+        in_specs=[vmem] * 3 + [hbm] * 3,
         out_specs=[hbm] * 2,
         out_shape=[
             jax.ShapeDtypeStruct((units, 4 * rows), BF),
@@ -299,7 +317,7 @@
             collective_id=0, has_side_effects=True, vmem_limit_bytes=60 << 20
         ),
         name="square_forward",
-    )(tokens, target, weight, live, w_gate, w_up, w_down)
+    )(tokens, target, weight, w_gate, w_up, w_down)
     return hidden_t, errors.reshape(4 * rows, width)
 
 

time: 178 us -> 164 us (0.921)
  other arithmetic: 8.71 us -> 0.66 us
  Pallas kernels: 167 us -> 161 us
    select_n x4 -> x1, other arithmetic: 7.31 us -> 0.66 us  [square_forward(): weight = jnp.where(row_ids < filled[0], combine.astype(F32), 0.0)[:, None]]
    pallas_call x3, Pallas kernels: 152 us -> 146 us  [the longest x1 124 us: square_forward(): pl.pallas_call(square_kernel, in_specs=[vmem] * 3 + [hbm] * 3, out_specs=...]
where the time goes in v2:
time: 164 us
  Pallas kernels  161 us (98%)
    pallas_call x1, Pallas kernels, square_forward(): pl.pallas_call(square_kernel, in_specs=[vmem] * 3 + [hbm] * 3, out_specs=...  124 us
    pallas_call x1, Pallas kernels, grad_step(): pl.pallas_call(functools.partial(grad_kernel, factor, subs), grid=(tiles,...  15.6 us
    pallas_call x1, Pallas kernels, band_sum(): pl.pallas_call(functools.partial(band_kernel, count), in_specs=[vmem], ou...  14.6 us
    pallas_call x1, Pallas kernels, update_step(): pl.pallas_call(functools.partial(update_kernel, replicas, subs), grid=(ti...  6.07 us

profile of v2, /device:TPU:0, one launch (start us, length us, event | category | flops | bytes accessed | tf_op | source)
XLA Modules:
  0.0 163.5 jit_solution(9801262823238834164)
XLA Ops:
  1.3 0.7 compare_select_fusion
  1.9 0.8 copy.18.weight
  2.7 124.5 %square_forward.1 = (bf16[512,1024]{1,0:T(8,128)(2,1)}, bf16[4,256,2304]{2,1,0:T(8,128)(2,1)}) custom-call(bf16[256,2304]{1,0:T(8,128)(2,1)} %tokens.1, bf16[256,2304]{1,0:T(8,128)(2,1)} %target.1, f32[256,1]{1,0:T(8,128)} %copy.18.weight, bf16[2304,512]{1,0:T(8,128)(2,1)} %gate_hbm.1, bf16[2304,512]{1,0:T(8,128)(2,1)} %up_hbm.1, bf16[512,2304]{1,0:T(8,128)(2,1)} %down_hbm.1), custom_call_target="tpu_custom_call" | custom-call | tf_op jit(solution)/shard_map/square_forward/pallas_call | solution.py:300
  127.2 15.6 %grad_step.1 = (f32[1,512,2304]{2,1,0:T(8,128)}, f32[576,128]{1,0:T(8,128)}) custom-call(bf16[512,1024]{1,0:T(8,128)(2,1)} %get-tuple-element.6.hidden_t, bf16[1024,2304]{1,0:T(8,128)(2,1)} %bitcast.4, f32[1,512,2304]{2,1,0:T(8,128)} %momentum.1, bf16[128,512]{1,0:T(8,128)(2,1)} %constant.24.clone.refs_0_, bf16[128,512]{1,0:T(8,128)(2,1)} %constant.25.clone.refs_1_, ...), custom_call_target="tpu_custom_call" | custom-call | tf_op jit(solution)/shard_map/grad_step/pallas_call | solution.py:73
  142.8 14.6 %band_sum.1.bands = f32[576,128]{1,0:T(8,128)} custom-call(f32[576,128]{1,0:T(8,128)} %get-tuple-element.9.band), custom_call_target="tpu_custom_call" | custom-call | tf_op jit(solution)/shard_map/band_sum/pallas_call | solution.py:359
  157.5 6.1 %update_step.1 = bf16[512,2304]{1,0:T(8,128)(2,1)} custom-call(f32[576,128]{1,0:T(8,128)} %band_sum.1.bands, bf16[128,512]{1,0:T(8,128)(2,1)} %constant.24.clone.refs_0_, bf16[128,512]{1,0:T(8,128)(2,1)} %constant.25.clone.refs_1_, bf16[512,128]{1,0:T(8,128)(2,1)} %constant.26.clone.refs_2_, bf16[512,128]{1,0:T(8,128)(2,1)} %constant.27.clone.refs_3_, ...), custom_call_target="tpu_custom_call" | custom-call | tf_op jit(solution)/shard_map/update_step/pallas_call | solution.py:109
